TPU v7x, 256 devices: a whole 4x4x8 slice. The times are simulated.
256 devices in a mesh: seq: 32 (over x, z), mlp: 8 (over y, core).
Axes of the slice: x: 4, y: 4, z: 8, core: 2. Of those that a mesh axis runs over, the one named last changes fastest.
Arguments:
- queries: bfloat16 [1024, 2560], P(('seq', 'mlp')), may hold values from -8 to 8
- new_kv: bfloat16 [1024, 512], P(('seq', 'mlp')), may hold values from -5 to 5
- kv_cache: bfloat16 [4352, 128, 512], P(('seq', 'mlp')), may hold values from -4 to 4, as said below
- lengths: int32 [256], replicated, may hold values from 256 to 16384, as said below
- page_table: int32 [256, 128], replicated, may hold values from -1 to 4351, as said below
- residual: bfloat16 [1024, 2560], P('seq', 'mlp'), may hold values from -3 to 3
- out_weight: bfloat16 [2560, 2560], P(None, 'mlp'), may hold values from -0.125 to 0.125
- norm_gain: float32 [2560], replicated, may hold values from 0.1 to 1.9
- gate_weight: bfloat16 [2560, 3840], P(None, 'mlp'), may hold values from -0.125 to 0.125
- up_weight: bfloat16 [2560, 3840], P(None, 'mlp'), may hold values from -0.125 to 0.125
- down_weight: bfloat16 [3840, 2560], P('mlp'), may hold values from -0.09375 to 0.09375
- next_gain: float32 [2560], replicated, may hold values from 0.1 to 1.9
- qkv_weight: bfloat16 [2560, 3072], P(None, 'mlp'), may hold values from -0.125 to 0.125
Outputs:
- attended: bfloat16 [1024, 2560], P(('seq', 'mlp'))
- residual_out: bfloat16 [1024, 2560], P('seq', 'mlp')
- next_qkv: bfloat16 [1024, 3072], P('seq', 'mlp')
Inputs may be any that keep to these rules, and one draw needn't show every extreme that they name: `lengths`: lengths have a heavy tail; at least one request has exactly 16384. page_table[r, p] is a slot exactly for the pages p holding positions max(0, lengths[r] - 2047) to lengths[r] - 1, and -1 elsewhere. Slots d * 17 to d * 17 + 16 lie on device d of seq+mlp. All pages of request r lie in consecutive slots of ONE device, whose mlp index is r modulo 8; a device may hold the pages of several requests or of none. No slot holds two pages; some device of every mlp index has all 17 slots in use. `kv_cache`: unused slots hold arbitrary values.
All inputs are finite; a program needn't handle non-finite values.
Results may differ from a plain program's by a relative error of at most 0.011.
Values may be sent and summed in bfloat16 or wider, within the bound.
No kernel may reach another device: no remote copies, remote signals or barrier semaphores. Data moves between devices by JAX's collectives and lax.ppermute only.
A program may use at most 64 MiB of HBM per device.

v0:
```python
import jax
import jax.numpy as jnp
from jax import lax
from jax.sharding import PartitionSpec as P

WINDOW = 2048
NEG_FILL = -1e30


def combine_parts(first, second):
    first_max, first_sum, first_acc = first
    second_max, second_sum, second_acc = second
    peak = jnp.maximum(first_max, second_max)
    first_factor = jnp.exp(first_max - peak)
    second_factor = jnp.exp(second_max - peak)
    return (
        peak,
        first_sum * first_factor + second_sum * second_factor,
        first_acc * first_factor[..., None] + second_acc * second_factor[..., None],
    )


def rms_norm(values, gain):
    floats = values.astype(jnp.float32)
    scaled = floats * lax.rsqrt(jnp.mean(floats * floats, axis=-1, keepdims=True) + 1e-06)
    return (scaled * gain).astype(jnp.bfloat16)


def shards(
    queries,
    new_kv,
    kv_cache,
    lengths,
    page_table,
    residual,
    out_weight,
    norm_gain,
    gate_weight,
    up_weight,
    down_weight,
    next_gain,
    qkv_weight,
):
    seq_count = lax.axis_size("seq")
    mlp_count = lax.axis_size("mlp")
    seq_place = lax.axis_index("seq")
    device = seq_place * mlp_count + lax.axis_index("mlp")
    slot_count = kv_cache.shape[0]
    page_len = kv_cache.shape[1]
    head_dim = kv_cache.shape[2] // 2
    token_count = queries.shape[0]
    width = queries.shape[1]
    head_count = width // head_dim
    request_total, page_count = page_table.shape
    scale = head_dim ** (-0.5)
    local_slot = page_table - device * slot_count
    inside = (local_slot >= 0) & (local_slot < slot_count)
    target = jnp.where(inside, local_slot, slot_count).reshape(-1)
    owners = jnp.broadcast_to(
        jnp.arange(request_total, dtype=jnp.int32)[:, None], page_table.shape
    ).reshape(-1)
    page_numbers = jnp.broadcast_to(
        jnp.arange(page_count, dtype=jnp.int32)[None, :], page_table.shape
    ).reshape(-1)
    slot_request = jnp.zeros((slot_count,), jnp.int32).at[target].set(owners, mode="drop")
    slot_page = jnp.zeros((slot_count,), jnp.int32).at[target].set(page_numbers, mode="drop")
    slot_used = jnp.zeros((slot_count,), jnp.bool_).at[target].set(True, mode="drop")
    column_rows = lax.all_gather(queries, "seq", axis=0, tiled=True)
    column_queries = column_rows.reshape(seq_count, token_count, head_count, head_dim)
    slot_column = slot_request // mlp_count
    slot_queries = column_queries[slot_column]
    cache_keys = kv_cache[:, :, :head_dim]
    cache_values = kv_cache[:, :, head_dim:]
    scores = (
        jnp.einsum("sqhd,skd->sqhk", slot_queries, cache_keys, preferred_element_type=jnp.float32)
        * scale
    )
    positions = slot_page[:, None] * page_len + jnp.arange(page_len, dtype=jnp.int32)[None, :]
    slot_length = lengths[slot_request]
    offsets = jnp.arange(token_count, dtype=jnp.int32)
    valid = (
        slot_used[:, None, None]
        & (positions[:, None, :] < slot_length[:, None, None])
        & (
            positions[:, None, :]
            >= slot_length[:, None, None] + offsets[None, :, None] - (WINDOW - 1)
        )
    )
    valid = valid[:, :, None, :]
    page_max = jnp.max(jnp.where(valid, scores, NEG_FILL), axis=-1)
    weights = jnp.where(valid, jnp.exp(scores - page_max[..., None]), 0.0)
    page_sum = jnp.sum(weights, axis=-1)
    page_acc = jnp.einsum(
        "sqhk,skd->sqhd",
        weights.astype(jnp.bfloat16),
        cache_values,
        preferred_element_type=jnp.float32,
    )
    member = (slot_column[None, :] == jnp.arange(seq_count, dtype=jnp.int32)[:, None]) & slot_used[
        None, :
    ]
    request_max = jnp.max(jnp.where(member[:, :, None, None], page_max[None], NEG_FILL), axis=1)
    rescale = jnp.exp(page_max - request_max[slot_column])
    member_float = member.astype(jnp.float32)
    request_sum = jnp.einsum(
        "rs,sqh->rqh", member_float, rescale * page_sum, precision=lax.Precision.HIGHEST
    )
    request_acc = jnp.einsum(
        "rs,sqhd->rqhd",
        member_float,
        rescale[..., None] * page_acc,
        precision=lax.Precision.HIGHEST,
    )
    got_max, got_sum, got_acc = (
        lax.all_to_all(request_max, "seq", split_axis=0, concat_axis=0, tiled=True),
        lax.all_to_all(request_sum, "seq", split_axis=0, concat_axis=0, tiled=True),
        lax.all_to_all(request_acc, "seq", split_axis=0, concat_axis=0, tiled=True),
    )
    peak = jnp.max(got_max, axis=0)
    factor = jnp.exp(got_max - peak[None])
    own_part = (
        peak,
        jnp.sum(factor * got_sum, axis=0),
        jnp.sum(factor[..., None] * got_acc, axis=0),
    )
    own_queries = queries.reshape(token_count, head_count, head_dim)
    new_keys = new_kv[:, :head_dim]
    new_values = new_kv[:, head_dim:]
    new_scores = (
        jnp.einsum("qhd,kd->qhk", own_queries, new_keys, preferred_element_type=jnp.float32) * scale
    )
    causal = (offsets[:, None] >= offsets[None, :])[:, None, :]
    new_max = jnp.max(jnp.where(causal, new_scores, NEG_FILL), axis=-1)
    new_weights = jnp.where(causal, jnp.exp(new_scores - new_max[..., None]), 0.0)
    new_sum = jnp.sum(new_weights, axis=-1)
    new_acc = jnp.einsum(
        "qhk,kd->qhd",
        new_weights.astype(jnp.bfloat16),
        new_values,
        preferred_element_type=jnp.float32,
    )
    final_max, final_sum, final_acc = combine_parts(own_part, (new_max, new_sum, new_acc))
    attended = (final_acc / final_sum[..., None]).reshape(token_count, width).astype(jnp.bfloat16)
    attention_out = jnp.dot(
        lax.all_gather(attended, "mlp", axis=0, tiled=True),
        out_weight,
        preferred_element_type=jnp.float32,
    )
    stream = (residual.astype(jnp.float32) + attention_out).astype(jnp.bfloat16)
    whole_stream = lax.all_gather(stream, "mlp", axis=1, tiled=True)
    normed = rms_norm(whole_stream, norm_gain)
    gate = jnp.dot(normed, gate_weight, preferred_element_type=jnp.float32)
    upward = jnp.dot(normed, up_weight, preferred_element_type=jnp.float32)
    hidden = (jax.nn.gelu(gate, approximate=True) * upward).astype(jnp.bfloat16)
    partial_down = jnp.dot(hidden, down_weight, preferred_element_type=jnp.float32)
    column_width = stream.shape[1]
    column_start = lax.axis_index("mlp") * column_width
    down_total = lax.psum(partial_down, "mlp")
    full_after = (whole_stream.astype(jnp.float32) + down_total).astype(jnp.bfloat16)
    shard_after = lax.dynamic_slice_in_dim(full_after, column_start, column_width, 1)
    normed_next = rms_norm(full_after, next_gain)
    next_qkv = jnp.dot(normed_next, qkv_weight, preferred_element_type=jnp.float32).astype(
        jnp.bfloat16
    )
    return (attended, shard_after, next_qkv)


def solution(mesh):
    return jax.shard_map(
        shards,
        mesh=mesh,
        in_specs=(
            P(("seq", "mlp"), None),
            P(("seq", "mlp"), None),
            P(("seq", "mlp"), None, None),
            P(),
            P(),
            P("seq", "mlp"),
            P(None, "mlp"),
            P(),
            P(None, "mlp"),
            P(None, "mlp"),
            P("mlp", None),
            P(),
            P(None, "mlp"),
        ),
        out_specs=(P(("seq", "mlp"), None), P("seq", "mlp"), P("seq", "mlp")),
        check_vma=False,
    )
```

profile of v0, /device:TPU:2, one launch (start us, length us, event | category | flops | bytes accessed | tf_op | source)
XLA Modules:
  0.0 617.3 jit_solution(3208878940347870312)
XLA Ops:
  7.2 0.0 copy-start
  7.2 1.1 and_select_fusion
  8.3 0.1 compare_select_fusion
  8.5 120.0 %scatter_custom_fusion = s32[17]{0:T(128)S(1)} fusion(s32[32768]{0:T(1024)S(1)} %bitcast.70, s32[32768]{0:T(1024)S(1)} %iota_bitcast_fusion.1, s32[]{:T(128)} %constant.28.clone.1), kind=kCustom, calls=%fused_computation.111 | custom fusion | bytes 72 | tf_op jit(solution)/shard_map/scatter | solution.py:65
  128.5 1.4 gather_fusion
  129.9 0.1 add_add_fusion
  130.0 120.0 %scatter_custom_fusion.2 = s32[17]{0:T(128)S(1)} fusion(s32[32768]{0:T(1024)S(1)} %bitcast.71, s32[32768]{0:T(1024)S(1)} %iota_bitcast_fusion, s32[]{:T(128)} %constant.28.clone.1), kind=kCustom, calls=%fused_computation.109 | custom fusion | bytes 72 | tf_op jit(solution)/shard_map/scatter | solution.py:66
  250.0 0.1 iota_add_fusion
  250.1 136.5 %scatter_custom_fusion.1 = pred[17]{0:T(512)(128)(4,1)S(1)} fusion(s32[32768]{0:T(1024)S(1)} %bitcast.72, pred[32768]{0:T(1024)(128)(4,1)S(1)} %broadcast.184, pred[]{:T(512)} %constant.20.clone.1), kind=kCustom, calls=%fused_computation.104 | custom fusion | bytes 18 | tf_op jit(solution)/shard_map/scatter | solution.py:67
  386.6 0.1 compare_and_fusion.1
  386.7 52.5 %all-gather = bf16[32,4,2560]{2,1,0:T(4,128)(2,1)S(1)} all-gather(bf16[1,4,2560]{2,1,0:T(4,128)(2,1)} %bitcast.74), channel_id=1, replica_groups=mesh['seq'=32,'mlp'=8] {'seq'}, dimensions={0}, use_global_device_ids=true | all-gather | bytes 675840 | tf_op jit(solution)/shard_map/all_gather | solution.py:68
  439.2 0.1 copy.49
  439.3 1.4 reshape.237
  440.7 2.7 gather_fusion.1
  443.3 0.1 compare_and_fusion
  443.4 2.0 select_reduce_fusion
  445.5 0.2 copy.50
  445.7 0.4 fusion.13
  446.1 0.1 fusion.43
  446.2 0.3 select_reduce_fusion.1
  446.5 0.7 copy.51
  447.2 1.4 gather_fusion.2
  448.6 0.2 fusion.37
  448.9 0.7 copy.58
  449.6 6.7 %all-to-all-start.2 = ((f32[32,4,10]{2,1,0:T(4,128)}), f32[32,4,10]{2,1,0:T(4,128)S(1)}, u32[]{:S(2)}, u32[]{:S(2)}) async-start(f32[32,4,10]{2,1,0:T(4,128)} %copy.58), calls=%async_computation.2 | async-start | bytes 131072 | tf_op jit(solution)/shard_map/all_to_all | solution.py:116
  456.3 2.7 convolution_multiply_fusion
  459.0 6.5 %all-to-all-done.2 = f32[32,4,10]{2,1,0:T(4,128)S(1)} async-done(((f32[32,4,10]{2,1,0:T(4,128)}), f32[32,4,10]{2,1,0:T(4,128)S(1)}, u32[]{:S(2)}, u32[]{:S(2)}) %all-to-all-start.2) | async-done | bytes 5152 | tf_op jit(solution)/shard_map/all_to_all | solution.py:116
  465.4 5.0 all-to-all-start
  470.4 2.3 fusion.11
  472.7 1.9 copy.55
  474.6 0.0 copy-start.1
  474.6 0.0 copy-start.5
  474.6 4.9 all-to-all-done
  479.6 6.7 %all-to-all-start.1 = ((f32[32,4,10,256]{3,1,2,0:T(4,128)}), f32[32,4,10,256]{3,1,2,0:T(4,128)}, u32[]{:S(2)}, u32[]{:S(2)}) async-start(f32[32,4,10,256]{3,1,2,0:T(4,128)} %copy.55), calls=%async_computation.1 | async-start | bytes 2621440 | tf_op jit(solution)/shard_map/all_to_all | solution.py:117
  486.3 0.0 copy-start.3
  486.3 0.0 all-reduce.2.cloned.1.call-start
  486.3 0.0 copy-done.1
  486.4 0.0 copy-done.5
  486.4 0.2 select_reduce_fusion.2
  486.5 0.1 fusion.46
  486.7 0.1 multiply_reduce_fusion.1
  486.7 0.3 copy.52
  487.1 18.4 %all-to-all-done.1 = f32[32,4,10,256]{3,1,2,0:T(4,128)} async-done(((f32[32,4,10,256]{3,1,2,0:T(4,128)}), f32[32,4,10,256]{3,1,2,0:T(4,128)}, u32[]{:S(2)}, u32[]{:S(2)}) %all-to-all-start.1) | async-done | bytes 1310752 | tf_op jit(solution)/shard_map/all_to_all | solution.py:117
  505.4 1.7 multiply_reduce_fusion
  507.1 0.3 fusion.3
  507.4 13.3 %all-gather.1 = bf16[8,4,2560]{2,1,0:T(4,128)(2,1)S(1)} all-gather(bf16[1,4,2560]{2,1,0:T(4,128)(2,1)S(1)} %reshape.292), channel_id=1, replica_groups=mesh['seq'=32,'mlp'=8] {'mlp'}, dimensions={0}, use_global_device_ids=true | all-gather | bytes 184320 | tf_op jit(solution)/shard_map/all_gather | solution.py:145
  520.8 0.0 copy-done.3
  520.8 2.0 fusion.10
  522.8 12.8 %all-gather.2 = bf16[8,320,32]{1,2,0:T(8,128)(2,1)S(1)} all-gather(bf16[1,320,32]{1,2,0:T(8,128)(2,1)S(1)} %fusion.10), channel_id=1, replica_groups=mesh['seq'=32,'mlp'=8] {'mlp'}, dimensions={0}, use_global_device_ids=true | all-gather | bytes 184320 | tf_op jit(solution)/shard_map/all_gather | solution.py:150
  535.6 0.1 copy.59
  535.7 0.1 reshape.298
  535.8 0.1 fusion.18
  535.9 0.0 copy-done.2
  536.0 2.5 fusion.74
  538.4 0.0 copy-done
  538.4 0.0 copy-start.4
  538.5 3.8 fusion.9
  542.2 0.0 all-reduce.2.cloned.1.call-update
  542.3 0.6 copy.63
  542.9 63.1 %all-reduce.2.cloned.1.call-done = f32[32,2560]{1,0:T(8,128)} async-done(((f32[32,2560]{1,0:T(8,128)}), f32[32,2560]{1,0:T(8,128)}) %all-reduce.2.cloned.1.call-update) | async-done | bytes 327696 | tf_op jit(solution)/shard_map/psum | solution.py:158
  606.0 1.1 fusion.15
  607.1 0.7 constant_dynamic-slice_fusion
  607.9 0.0 copy-done.4
  607.9 2.6 convolution_convert_fusion
  (17 shorter events, 0.2 us)
Async XLA Ops:
  7.2 531.3 %copy-start = (bf16[480,2560]{1,0:T(8,128)(2,1)S(1)}, bf16[480,2560]{1,0:T(8,128)(2,1)}, u32[]{:S(2)}) copy-start(bf16[480,2560]{1,0:T(8,128)(2,1)} %param.23) | copy-start | bytes 7372804
  449.6 15.8 %all-to-all-start.2 = ((f32[32,4,10]{2,1,0:T(4,128)}), f32[32,4,10]{2,1,0:T(4,128)S(1)}, u32[]{:S(2)}, u32[]{:S(2)}) async-start(f32[32,4,10]{2,1,0:T(4,128)} %copy.58), calls=%async_computation.2 | async-start | bytes 131072 | tf_op jit(solution)/shard_map/all_to_all | solution.py:116
  465.4 14.2 %all-to-all-start = ((f32[32,4,10]{2,1,0:T(4,128)}), f32[32,4,10]{2,1,0:T(4,128)S(1)}, u32[]{:S(2)}, u32[]{:S(2)}) async-start(f32[32,4,10]{2,1,0:T(4,128)} %copy.51), calls=%async_computation | async-start | bytes 131072 | tf_op jit(solution)/shard_map/all_to_all | solution.py:115
  474.6 11.7 %copy-start.1 = (bf16[4,2560]{1,0:T(4,128)(2,1)S(1)}, bf16[4,2560]{1,0:T(4,128)(2,1)}, u32[]{:S(2)}) copy-start(bf16[4,2560]{1,0:T(4,128)(2,1)} %param.13) | copy-start | bytes 61444
  474.6 11.7 %copy-start.5 = (bf16[4,512]{1,0:T(4,128)(2,1)S(1)}, bf16[4,512]{1,0:T(4,128)(2,1)}, u32[]{:S(2)}) copy-start(bf16[4,512]{1,0:T(4,128)(2,1)} %param.14) | copy-start | bytes 12292
  479.6 25.8 %all-to-all-start.1 = ((f32[32,4,10,256]{3,1,2,0:T(4,128)}), f32[32,4,10,256]{3,1,2,0:T(4,128)}, u32[]{:S(2)}, u32[]{:S(2)}) async-start(f32[32,4,10,256]{3,1,2,0:T(4,128)} %copy.55), calls=%async_computation.1 | async-start | bytes 2621440 | tf_op jit(solution)/shard_map/all_to_all | solution.py:117
  486.3 34.5 %copy-start.3 = (bf16[32,320]{1,0:T(8,128)(2,1)S(1)}, bf16[32,320]{1,0:T(8,128)(2,1)}, u32[]{:S(2)}) copy-start(bf16[32,320]{1,0:T(8,128)(2,1)} %param.18) | copy-start | bytes 61444
  486.3 119.8 %all-reduce.2.cloned.1.call-start = ((), (), s32[]{:S(2)}) async-start(), calls=%async_computation.3 | async-start | bytes 655360 | tf_op jit(solution)/shard_map/psum | solution.py:158
  520.7 15.2 %copy-start.2 = (f32[2560]{0:T(1024)S(1)}, f32[2560]{0:T(1024)}, u32[]{:S(2)}) copy-start(f32[2560]{0:T(1024)} %param.20) | copy-start | bytes 30724
  538.4 69.4 %copy-start.4 = (f32[2560]{0:T(1024)S(1)}, f32[2560]{0:T(1024)}, u32[]{:S(2)}) copy-start(f32[2560]{0:T(1024)} %param.24) | copy-start | bytes 30724
Sparse Core Ops, SparseCore 0:
  542.4 63.6 all-reduce.1
where the time goes:
time: 618 us; the launch traced here: 617 us
  local copies, waits for them, and re-layouts  389 us (63%)
  waiting for transfers between devices  92.9 us (15%)
  blocking collectives  78.6 us (13%)
  matrix products  18.6 us (3%)
  starting transfers between devices  18.3 us (3%)
  between operations  14.3 us (2%)
    scatter x1, local copies, waits for them, and re-layouts, shards(): jnp.zeros((slot_count,), jnp.bool_).at[target].set(True, mode='drop')  136 us
    scatter x1, local copies, waits for them, and re-layouts, shards(): jnp.zeros((slot_count,), jnp.int32).at[target].set(owners, mode='drop')  120 us
    scatter x1, local copies, waits for them, and re-layouts, shards(): jnp.zeros((slot_count,), jnp.int32).at[target]  120 us
    psum x1, waiting for transfers between devices, shards(): down_total = lax.psum(partial_down, 'mlp')  63.1 us
    all_gather x1, blocking collectives, shards(): column_rows = lax.all_gather(queries, 'seq', axis=0, tiled=True)  52.5 us
    all_to_all x1, waiting for transfers between devices, shards(): lax.all_to_all(request_acc, 'seq', split_axis=0, concat_axis=0, tiled=True)  18.4 us
    all_gather x1, blocking collectives, shards(): lax.all_gather(attended, 'mlp', axis=0, tiled=True)  13.3 us
    all_gather x1, blocking collectives, shards(): whole_stream = lax.all_gather(stream, 'mlp', axis=1, tiled=True)  12.8 us
  transfers between devices with their start and end apart: 4, of which 4 were waited for; matrix products, arithmetic and copies ran while one was open for 1% of the time, Pallas kernels for 0%

commit v1 on v0

--- a/solution.py
+++ b/solution.py
@@ -155,7 +155,11 @@
     partial_down = jnp.dot(hidden, down_weight, preferred_element_type=jnp.float32)
     column_width = stream.shape[1]
     column_start = lax.axis_index("mlp") * column_width
-    down_total = lax.psum(partial_down, "mlp")
+    down_total = partial_down
+    for hop in (1, 2, 4):
+        down_total = down_total + lax.ppermute(
+            down_total, "mlp", [(dev, dev ^ hop) for dev in range(8)]
+        )
     full_after = (whole_stream.astype(jnp.float32) + down_total).astype(jnp.bfloat16)
     shard_after = lax.dynamic_slice_in_dim(full_after, column_start, column_width, 1)
     normed_next = rms_norm(full_after, next_gain)

time: 618 us -> 564 us (0.913)
  waiting for transfers between devices: 92.9 us -> 47.6 us
  between operations: 14.3 us -> 0.91 us
    psum x1 -> x0, waiting for transfers between devices: 63.1 us -> none  [shards(): down_total = lax.psum(partial_down, 'mlp')]
    ppermute x0 -> x3, waiting for transfers between devices: none -> 17.8 us  [shards(): lax.ppermute(down_total, 'mlp', [(dev, dev ^ hop) for dev in range(8)])]
  transfers between devices with their start and end apart: 4 -> 6, of which waited for: 4 -> 6; matrix products, arithmetic and copies ran while one was open for 1% -> 1% of each run, Pallas kernels for 0% -> 0%
where the time goes in v1:
time: 564 us; the launch traced here: 561 us
  local copies, waits for them, and re-layouts  389 us (69%)
  blocking collectives  78.6 us (14%)
  waiting for transfers between devices  47.6 us (8%)
  starting transfers between devices  22.3 us (4%)
  matrix products  17.8 us (3%)
    scatter x1, local copies, waits for them, and re-layouts, shards(): jnp.zeros((slot_count,), jnp.bool_).at[target].set(True, mode='drop')  136 us
    scatter x1, local copies, waits for them, and re-layouts, shards(): jnp.zeros((slot_count,), jnp.int32).at[target].set(owners, mode='drop')  120 us
    scatter x1, local copies, waits for them, and re-layouts, shards(): jnp.zeros((slot_count,), jnp.int32).at[target]  120 us
    all_gather x1, blocking collectives, shards(): column_rows = lax.all_gather(queries, 'seq', axis=0, tiled=True)  52.5 us
    all_to_all x1, waiting for transfers between devices, shards(): lax.all_to_all(request_acc, 'seq', split_axis=0, concat_axis=0, tiled=True)  18.4 us
    ppermute x3, waiting for transfers between devices, shards(): lax.ppermute(down_total, 'mlp', [(dev, dev ^ hop) for dev in range(8)])  17.8 us
    all_gather x1, blocking collectives, shards(): lax.all_gather(attended, 'mlp', axis=0, tiled=True)  13.3 us
    all_gather x1, blocking collectives, shards(): whole_stream = lax.all_gather(stream, 'mlp', axis=1, tiled=True)  12.8 us
  transfers between devices with their start and end apart: 6, of which 6 were waited for; matrix products, arithmetic and copies ran while one was open for 1% of the time, Pallas kernels for 0%

profile of v1, /device:TPU:2, one launch (start us, length us, event | category | flops | bytes accessed | tf_op | source)
XLA Modules:
  0.0 561.0 jit_solution(3437485846444948376)
XLA Ops:
  0.6 0.0 copy-start
  0.7 1.1 and_select_fusion
  1.8 0.1 compare_select_fusion
  1.9 120.0 %scatter_custom_fusion = s32[17]{0:T(128)S(1)} fusion(s32[32768]{0:T(1024)S(1)} %bitcast.70, s32[32768]{0:T(1024)S(1)} %iota_bitcast_fusion.1, s32[]{:T(128)} %constant.28.clone.1), kind=kCustom, calls=%fused_computation.111 | custom fusion | bytes 72 | tf_op jit(solution)/shard_map/scatter | solution.py:65
  122.0 1.4 gather_fusion
  123.4 0.1 add_add_fusion
  123.4 120.0 %scatter_custom_fusion.2 = s32[17]{0:T(128)S(1)} fusion(s32[32768]{0:T(1024)S(1)} %bitcast.71, s32[32768]{0:T(1024)S(1)} %iota_bitcast_fusion, s32[]{:T(128)} %constant.28.clone.1), kind=kCustom, calls=%fused_computation.109 | custom fusion | bytes 72 | tf_op jit(solution)/shard_map/scatter | solution.py:66
  243.5 0.1 iota_add_fusion
  243.6 136.5 %scatter_custom_fusion.1 = pred[17]{0:T(512)(128)(4,1)S(1)} fusion(s32[32768]{0:T(1024)S(1)} %bitcast.72, pred[32768]{0:T(1024)(128)(4,1)S(1)} %broadcast.184, pred[]{:T(512)} %constant.20.clone.1), kind=kCustom, calls=%fused_computation.104 | custom fusion | bytes 18 | tf_op jit(solution)/shard_map/scatter | solution.py:67
  380.1 0.1 compare_and_fusion.1
  380.1 52.5 %all-gather = bf16[32,4,2560]{2,1,0:T(4,128)(2,1)S(1)} all-gather(bf16[1,4,2560]{2,1,0:T(4,128)(2,1)} %bitcast.74), channel_id=1, replica_groups=mesh['seq'=32,'mlp'=8] {'seq'}, dimensions={0}, use_global_device_ids=true | all-gather | bytes 675840 | tf_op jit(solution)/shard_map/all_gather | solution.py:68
  432.6 0.1 copy.49
  432.8 1.4 reshape.237
  434.1 2.7 gather_fusion.1
  436.8 0.1 compare_and_fusion
  436.9 2.0 select_reduce_fusion
  438.9 0.2 copy.50
  439.2 0.4 fusion.13
  439.6 0.1 fusion.43
  439.7 0.3 select_reduce_fusion.1
  439.9 0.7 copy.51
  440.7 1.4 gather_fusion.2
  442.1 0.2 fusion.37
  442.4 0.7 copy.58
  443.1 6.7 %all-to-all-start.2 = ((f32[32,4,10]{2,1,0:T(4,128)}), f32[32,4,10]{2,1,0:T(4,128)S(1)}, u32[]{:S(2)}, u32[]{:S(2)}) async-start(f32[32,4,10]{2,1,0:T(4,128)} %copy.58), calls=%async_computation.2 | async-start | bytes 131072 | tf_op jit(solution)/shard_map/all_to_all | solution.py:116
  449.8 2.7 convolution_multiply_fusion
  452.4 6.5 %all-to-all-done.2 = f32[32,4,10]{2,1,0:T(4,128)S(1)} async-done(((f32[32,4,10]{2,1,0:T(4,128)}), f32[32,4,10]{2,1,0:T(4,128)S(1)}, u32[]{:S(2)}, u32[]{:S(2)}) %all-to-all-start.2) | async-done | bytes 5152 | tf_op jit(solution)/shard_map/all_to_all | solution.py:116
  458.9 5.0 all-to-all-start
  463.9 2.3 fusion.11
  466.2 1.9 copy.55
  468.1 4.9 all-to-all-done
  473.1 6.7 %all-to-all-start.1 = ((f32[32,4,10,256]{3,1,2,0:T(4,128)}), f32[32,4,10,256]{3,1,2,0:T(4,128)}, u32[]{:S(2)}, u32[]{:S(2)}) async-start(f32[32,4,10,256]{3,1,2,0:T(4,128)} %copy.55), calls=%async_computation.1 | async-start | bytes 2621440 | tf_op jit(solution)/shard_map/all_to_all | solution.py:117
  479.7 0.0 copy-done.1
  479.7 0.0 copy-start.3
  479.8 0.0 copy-done.5
  479.8 0.2 select_reduce_fusion.2
  480.0 0.1 fusion.46
  480.1 0.1 multiply_reduce_fusion.1
  480.2 0.3 copy.52
  480.5 18.4 %all-to-all-done.1 = f32[32,4,10,256]{3,1,2,0:T(4,128)} async-done(((f32[32,4,10,256]{3,1,2,0:T(4,128)}), f32[32,4,10,256]{3,1,2,0:T(4,128)}, u32[]{:S(2)}, u32[]{:S(2)}) %all-to-all-start.1) | async-done | bytes 1310752 | tf_op jit(solution)/shard_map/all_to_all | solution.py:117
  498.9 1.7 multiply_reduce_fusion
  500.6 0.3 fusion.3
  500.9 13.3 %all-gather.1 = bf16[8,4,2560]{2,1,0:T(4,128)(2,1)S(1)} all-gather(bf16[1,4,2560]{2,1,0:T(4,128)(2,1)S(1)} %reshape.292), channel_id=1, replica_groups=mesh['seq'=32,'mlp'=8] {'mlp'}, dimensions={0}, use_global_device_ids=true | all-gather | bytes 184320 | tf_op jit(solution)/shard_map/all_gather | solution.py:145
  514.3 0.0 copy-done.3
  514.3 2.0 fusion.10
  516.3 12.8 %all-gather.2 = bf16[8,320,32]{1,2,0:T(8,128)(2,1)S(1)} all-gather(bf16[1,320,32]{1,2,0:T(8,128)(2,1)S(1)} %fusion.10), channel_id=1, replica_groups=mesh['seq'=32,'mlp'=8] {'mlp'}, dimensions={0}, use_global_device_ids=true | all-gather | bytes 184320 | tf_op jit(solution)/shard_map/all_gather | solution.py:150
  529.1 0.1 copy.59
  529.1 0.1 reshape.298
  529.3 0.1 fusion.18
  529.4 0.0 copy-done.2
  529.4 2.5 fusion.74
  531.9 0.0 copy-done
  531.9 3.0 fusion.9
  534.9 0.4 collective-permute-start
  535.3 1.3 collective-permute-done
  536.6 0.1 add.137
  536.7 1.4 collective-permute-start.1
  538.0 8.7 %collective-permute-done.1 = f32[32,2560]{1,0:T(8,128)S(1)} collective-permute-done((f32[32,2560]{1,0:T(8,128)S(1)}, f32[32,2560]{1,0:T(8,128)S(1)}, u32[]{:S(2)}, u32[]{:S(2)}) %collective-permute-start.1) | collective-permute-done | bytes 327712 | tf_op jit(solution)/shard_map/ppermute | solution.py:160
  546.8 2.3 collective-permute-start.2
  549.1 0.6 copy.63
  549.7 7.8 %collective-permute-done.2 = f32[32,2560]{1,0:T(8,128)S(1)} collective-permute-done((f32[32,2560]{1,0:T(8,128)S(1)}, f32[32,2560]{1,0:T(8,128)S(1)}, u32[]{:S(2)}, u32[]{:S(2)}) %collective-permute-start.2) | collective-permute-done | bytes 327712 | tf_op jit(solution)/shard_map/ppermute | solution.py:160
  557.5 0.2 fusion.15
  557.7 0.7 constant_dynamic-slice_fusion
  558.4 2.6 convolution_convert_fusion
  (22 shorter events, 0.3 us)
Async XLA Ops:
  0.6 531.3 %copy-start = (bf16[480,2560]{1,0:T(8,128)(2,1)S(1)}, bf16[480,2560]{1,0:T(8,128)(2,1)}, u32[]{:S(2)}) copy-start(bf16[480,2560]{1,0:T(8,128)(2,1)} %param.23) | copy-start | bytes 7372804
  443.1 15.8 %all-to-all-start.2 = ((f32[32,4,10]{2,1,0:T(4,128)}), f32[32,4,10]{2,1,0:T(4,128)S(1)}, u32[]{:S(2)}, u32[]{:S(2)}) async-start(f32[32,4,10]{2,1,0:T(4,128)} %copy.58), calls=%async_computation.2 | async-start | bytes 131072 | tf_op jit(solution)/shard_map/all_to_all | solution.py:116
  458.9 14.2 %all-to-all-start = ((f32[32,4,10]{2,1,0:T(4,128)}), f32[32,4,10]{2,1,0:T(4,128)S(1)}, u32[]{:S(2)}, u32[]{:S(2)}) async-start(f32[32,4,10]{2,1,0:T(4,128)} %copy.51), calls=%async_computation | async-start | bytes 131072 | tf_op jit(solution)/shard_map/all_to_all | solution.py:115
  468.1 11.6 %copy-start.1 = (bf16[4,2560]{1,0:T(4,128)(2,1)S(1)}, bf16[4,2560]{1,0:T(4,128)(2,1)}, u32[]{:S(2)}) copy-start(bf16[4,2560]{1,0:T(4,128)(2,1)} %param.13) | copy-start | bytes 61444
  468.1 11.7 %copy-start.5 = (bf16[4,512]{1,0:T(4,128)(2,1)S(1)}, bf16[4,512]{1,0:T(4,128)(2,1)}, u32[]{:S(2)}) copy-start(bf16[4,512]{1,0:T(4,128)(2,1)} %param.14) | copy-start | bytes 12292
  473.1 25.8 %all-to-all-start.1 = ((f32[32,4,10,256]{3,1,2,0:T(4,128)}), f32[32,4,10,256]{3,1,2,0:T(4,128)}, u32[]{:S(2)}, u32[]{:S(2)}) async-start(f32[32,4,10,256]{3,1,2,0:T(4,128)} %copy.55), calls=%async_computation.1 | async-start | bytes 2621440 | tf_op jit(solution)/shard_map/all_to_all | solution.py:117
  479.7 34.5 %copy-start.3 = (bf16[32,320]{1,0:T(8,128)(2,1)S(1)}, bf16[32,320]{1,0:T(8,128)(2,1)}, u32[]{:S(2)}) copy-start(bf16[32,320]{1,0:T(8,128)(2,1)} %param.18) | copy-start | bytes 61444
  514.2 15.2 %copy-start.2 = (f32[2560]{0:T(1024)S(1)}, f32[2560]{0:T(1024)}, u32[]{:S(2)}) copy-start(f32[2560]{0:T(1024)} %param.20) | copy-start | bytes 30724
  534.9 23.5 %copy-start.4 = (f32[2560]{0:T(1024)S(1)}, f32[2560]{0:T(1024)}, u32[]{:S(2)}) copy-start(f32[2560]{0:T(1024)} %param.24) | copy-start | bytes 30724
  534.9 1.7 collective-permute-start
  536.7 10.0 %collective-permute-start.1 = (f32[32,2560]{1,0:T(8,128)S(1)}, f32[32,2560]{1,0:T(8,128)S(1)}, u32[]{:S(2)}, u32[]{:S(2)}) collective-permute-start(f32[32,2560]{1,0:T(8,128)S(1)} %add.137), channel_id=1, source_target_pairs={{0,2},{1,3},{2,0},{3,1},{4,6},{5,7},{6,4},{7,5},{8,10},{9,11},{10,... | collective-permute-start | bytes 983048 | tf_op jit(solution)/shard_map/ppermute | solution.py:160
  546.8 10.7 %collective-permute-start.2 = (f32[32,2560]{1,0:T(8,128)S(1)}, f32[32,2560]{1,0:T(8,128)S(1)}, u32[]{:S(2)}, u32[]{:S(2)}) collective-permute-start(f32[32,2560]{1,0:T(8,128)S(1)} %add.138), channel_id=1, source_target_pairs={{0,4},{1,5},{2,6},{3,7},{4,0},{5,1},{6,2},{7,3},{8,12},{9,13},{10,... | collective-permute-start | bytes 983048 | tf_op jit(solution)/shard_map/ppermute | solution.py:160
